TPU v7x, 32 devices: a whole 2x2x4 slice. The times are simulated.
32 devices in a mesh: snap: 8 (over z, y), ord: 4 (over x, core).
Axes of the slice: x: 2, y: 2, z: 4, core: 2. Of those that a mesh axis runs over, the one named last changes fastest.
Arguments:
- images: bfloat16 [512, 256, 1024], P(('snap', 'ord')), may hold values from -8 to 8
- cycle_masks: int32 [512, 256], P('snap'), may hold values from 0 to 1, as said below
- weights: float32 [512], P('snap'), may hold values from 1 to 4
- inversion: float32 [128, 128], replicated, may hold values from -1 to 2
Outputs:
- kam: float32 [128, 256, 256], P('ord', 'snap')
Inputs may be any that keep to these rules, and one draw needn't show every extreme that they name: `cycle_masks`: each entry is 0 or 1; the same 4 cycles, drawn from the seed, are 0 in every snapshot.
All inputs are finite; a program needn't handle non-finite values.
Results may differ from a plain program's by a relative error of at most 0.0015.
Values may be sent and summed in bfloat16 or wider, within the bound.
No kernel may reach another device: no remote copies, remote signals or barrier semaphores. Data moves between devices by JAX's collectives and lax.ppermute only.
A program may use at most 64 MiB of HBM per device.

v0:
```python
import math

import jax
import jax.numpy as jnp
from jax import lax
from jax.sharding import PartitionSpec as P


def make_table(orders, angles):
    order_index = jnp.arange(orders, dtype=jnp.int32)
    angle_index = jnp.arange(angles, dtype=jnp.int32)
    phase_index = order_index[:, None] * angle_index[None, :] % angles
    radians = phase_index.astype(jnp.float32) * (2.0 * math.pi / angles)
    norming = math.sqrt(2.0 / angles)
    return jnp.concatenate(
        [jnp.cos(radians) * norming, -jnp.sin(radians) * norming], axis=0
    ).astype(jnp.bfloat16)


def weighted_gram(arrived, weight_rows):
    weighted = (arrived.astype(jnp.float32) * weight_rows[None, None, :, None]).astype(jnp.bfloat16)
    return jnp.einsum("rlsq,rlsp->lqp", weighted, arrived, preferred_element_type=jnp.float32)


def on_device(images, cycle_masks, weights, inversion):
    snap_dev, cycle_count, angles = images.shape
    orders = inversion.shape[0]
    snap_size = lax.axis_size("snap")
    ord_size = lax.axis_size("ord")
    ord_index = lax.axis_index("ord")
    dft_table = make_table(orders, angles)
    group_masks = cycle_masks.astype(jnp.float32)
    own_masks = lax.dynamic_slice_in_dim(group_masks, ord_index * snap_dev, snap_dev, 0)
    coeffs = jnp.einsum("ka,sqa->ksq", dft_table, images, preferred_element_type=jnp.float32)
    coeffs = (
        (coeffs * own_masks[None]).astype(jnp.bfloat16).reshape(2, orders, snap_dev, cycle_count)
    )
    masked_weight = group_masks * weights[:, None]
    partial_count = jnp.einsum(
        "sq,sp->qp", masked_weight, group_masks, precision=lax.Precision.HIGHEST
    )
    per_device = orders // (snap_size * ord_size)
    shaped = coeffs.reshape(2, ord_size, snap_size * per_device, snap_dev, cycle_count)
    arrived = lax.all_to_all(
        lax.all_to_all(shaped, "snap", split_axis=2, concat_axis=3, tiled=True),
        "ord",
        split_axis=1,
        concat_axis=3,
        tiled=True,
    )
    arrived = arrived.reshape(2, per_device, -1, cycle_count)
    weight_all = lax.all_gather(weights, "snap", axis=0, tiled=True)
    weight_all = weight_all.reshape(snap_size, ord_size, snap_dev).transpose(1, 0, 2).reshape(-1)
    partial_value = weighted_gram(arrived, weight_all)
    gram_sum = lax.all_to_all(partial_value, "snap", split_axis=1, concat_axis=0, tiled=True)
    pair_count = lax.psum_scatter(partial_count, "snap", scatter_dimension=0, tiled=True)
    correl = gram_sum / jnp.maximum(pair_count, 1.0)[None]
    local_orders = correl.shape[0]
    own_rows = lax.dynamic_slice_in_dim(inversion, ord_index * local_orders, local_orders, 0)
    return jnp.einsum(
        "ln,nqp->lqp",
        own_rows,
        lax.all_gather(correl, "ord", axis=0, tiled=True),
        precision=lax.Precision.HIGHEST,
    )


def solution(mesh):
    placed = (P(("snap", "ord"), None, None), P("snap", None), P("snap"), P())
    return jax.shard_map(
        on_device, mesh=mesh, in_specs=placed, out_specs=P("ord", "snap", None), check_vma=False
    )
```

profile of v0, /device:TPU:0, one launch (start us, length us, event | category | flops | bytes accessed | tf_op | source)
XLA Modules:
  0.0 228.0 jit_solution(37374247902323197)
XLA Ops:
  6.5 0.0 copy-start
  6.5 2.2 multiply_convert_fusion.5
  8.7 0.8 convert_element_type.19
  9.6 5.8 %multiply_convert_fusion.1 = bf16[256,16,256]{2,0,1:T(8,128)(2,1)S(1)} fusion(bf16[16,256,1024]{2,1,0:T(8,128)(2,1)} %param.4, f32[16,256]{1,0:T(8,128)S(1)} %constant_dynamic-slice_fusion, bf16[128,1024]{1,0:T(8,128)(2,1)S(1)} %get-tuple-element.5, bf16[128,1024]{1,0:T(8,128)(2,1)S(1)} %get-tuple-element.6), kind=kOutput, calls=%fused_computation.1 | convolution fusion | flops 2150629376 | bytes 11026432 | tf_op jit(solution)/shard_map/ka,sqa->ksq/dot_general | solution.py:34
  15.3 1.6 copy.18
  17.0 55.3 %all_to_all.51 = bf16[2,4,32,16,256]{4,1,0,3,2:T(4,128)(2,1)S(1)} all-to-all(bf16[2,4,32,16,256]{4,1,0,3,2:T(4,128)(2,1)S(1)} %copy.18), channel_id=1, replica_groups=mesh['snap'=8,'ord'=4] {'snap'}, dimensions={2} | all-to-all | bytes 4194304 | tf_op jit(solution)/shard_map/all_to_all | solution.py:45
  72.3 0.0 copy-start.3
  72.3 0.0 copy-start.2
  72.3 1.8 copy.19
  74.1 3.6 %all-to-all-start.1 = ((bf16[2,4,4,128,256]{4,3,0,2,1:T(8,128)(2,1)}), bf16[2,4,4,128,256]{4,3,0,2,1:T(8,128)(2,1)S(1)}, u32[]{:S(2)}, u32[]{:S(2)}) async-start(bf16[2,4,4,128,256]{4,3,0,2,1:T(8,128)(2,1)} %bitcast.31), calls=%async_computation.1 | async-start | bytes 4194304 | tf_op jit(solution)/shard_map/all_to_all | solution.py:44
  77.8 0.0 copy-done.3
  77.8 0.6 dynamic-slice
  79.0 0.0 copy-done.2
  79.0 0.2 dynamic-update-slice
  79.3 19.4 %all-reduce = f32[512]{0:T(512)S(1)} all-reduce(f32[512]{0:T(512)S(1)} %dynamic-update-slice), channel_id=1, replica_groups=mesh['snap'=8,'ord'=4] {'snap'}, use_global_device_ids=true, to_apply=%add | all-reduce | flops 512 | bytes 4096
  98.7 0.1 reshape.12
  98.8 0.1 mul.76
  98.9 4.5 %all-to-all-done.1 = bf16[2,4,4,128,256]{4,3,0,2,1:T(8,128)(2,1)S(1)} async-done(((bf16[2,4,4,128,256]{4,3,0,2,1:T(8,128)(2,1)}), bf16[2,4,4,128,256]{4,3,0,2,1:T(8,128)(2,1)S(1)}, u32[]{:S(2)}, u32[]{:S(2)}) %all-to-all-start.1) | async-done | bytes 2097184 | tf_op jit(solution)/shard_map/all_to_all | solution.py:44
  103.4 0.1 copy.20
  103.5 0.0 copy-start.1
  103.5 1.2 fusion.2
  104.8 1.6 copy.23
  106.4 3.6 %all-to-all-start.2 = ((f32[4,256,256]{2,0,1:T(4,128)}), f32[4,256,256]{2,0,1:T(4,128)S(1)}, u32[]{:S(2)}, u32[]{:S(2)}) async-start(f32[4,256,256]{2,0,1:T(4,128)} %copy.23), calls=%async_computation.2 | async-start | bytes 2097152 | tf_op jit(solution)/shard_map/all_to_all | solution.py:55
  110.0 0.0 reduce-scatter.2.cloned.1.call-start
  110.0 0.0 copy-done.1
  110.1 1.2 fusion.11
  111.2 0.0 reduce-scatter.2.cloned.1.call-update
  111.3 0.0 all-gather.2.cloned.1.call-start
  111.3 68.1 %reduce-scatter.2.cloned.1.call-done = f32[32,256]{1,0:T(8,128)} async-done(((f32[256,256]{1,0:T(8,128)}), f32[32,256]{1,0:T(8,128)}) %reduce-scatter.2.cloned.1.call-update) | async-done | bytes 32784 | tf_op jit(solution)/shard_map/reduce_scatter | solution.py:56
  179.4 0.8 broadcast_maximum_fusion
  180.2 0.0 all-to-all-done.2
  180.2 0.3 copy.29
  180.5 0.4 all_to_all.47
  180.9 1.1 broadcast_divide_fusion
  181.9 0.0 all-gather.2.cloned.1.call-update
  182.0 33.6 %all-gather.2.cloned.1.call-done = f32[128,32,256]{2,0,1:T(8,128)} async-done(((f32[32,32,256]{2,0,1:T(8,128)}), f32[128,32,256]{2,0,1:T(8,128)}) %all-gather.2.cloned.1.call-update) | async-done | bytes 4194320 | tf_op jit(solution)/shard_map/all_gather | solution.py:63
  215.6 0.0 copy-done
  215.6 4.0 %fusion.14 = f32[32,32,256]{2,0,1:T(8,128)S(1)} fusion(f32[128,32,256]{2,0,1:T(8,128)} %all-gather.2.cloned.1.call-done, f32[128,128]{1,0:T(8,128)S(1)} %copy-done, s32[]{:T(128)S(6)} %select_n.15), kind=kOutput, calls=%fused_computation.24 | convolution fusion | flops 402653184 | bytes 5259268 | tf_op jit(solution)/shard_map/ln,nqp->lqp/dot_general | solution.py:60
  219.6 1.6 copy.25
  (3 shorter events, 0.0 us)
Async XLA Ops:
  6.5 209.1 %copy-start = (f32[128,128]{1,0:T(8,128)S(1)}, f32[128,128]{1,0:T(8,128)}, u32[]{:S(2)}) copy-start(f32[128,128]{1,0:T(8,128)} %param.7) | copy-start | bytes 196612
  72.3 5.4 %copy-start.3 = (u32[32]{0:T(128)S(1)}, u32[32]{0:T(128)}, u32[]{:S(2)}) copy-start(u32[32]{0:T(128)} %constant.37) | copy-start | bytes 388
  72.3 6.7 %copy-start.2 = (f32[64]{0:T(128)S(1)}, f32[64]{0:T(128)}, u32[]{:S(2)}) copy-start(f32[64]{0:T(128)} %param.6) | copy-start | bytes 772
  74.1 29.2 %all-to-all-start.1 = ((bf16[2,4,4,128,256]{4,3,0,2,1:T(8,128)(2,1)}), bf16[2,4,4,128,256]{4,3,0,2,1:T(8,128)(2,1)S(1)}, u32[]{:S(2)}, u32[]{:S(2)}) async-start(bf16[2,4,4,128,256]{4,3,0,2,1:T(8,128)(2,1)} %bitcast.31), calls=%async_computation.1 | async-start | bytes 4194304 | tf_op jit(solution)/shard_map/all_to_all | solution.py:44
  103.5 6.5 %copy-start.1 = (s32[64,256]{1,0:T(8,128)S(1)}, s32[64,256]{1,0:T(8,128)}, u32[]{:S(2)}) copy-start(s32[64,256]{1,0:T(8,128)} %param.5) | copy-start | bytes 196612
  106.4 73.8 %all-to-all-start.2 = ((f32[4,256,256]{2,0,1:T(4,128)}), f32[4,256,256]{2,0,1:T(4,128)S(1)}, u32[]{:S(2)}, u32[]{:S(2)}) async-start(f32[4,256,256]{2,0,1:T(4,128)} %copy.23), calls=%async_computation.2 | async-start | bytes 2097152 | tf_op jit(solution)/shard_map/all_to_all | solution.py:55
  110.0 69.4 %reduce-scatter.2.cloned.1.call-start = ((), (), s32[]{:S(2)}) async-start(), calls=%async_computation.4 | async-start | bytes 294912 | tf_op jit(solution)/shard_map/reduce_scatter | solution.py:56
  111.3 104.3 %all-gather.2.cloned.1.call-start = ((), (), s32[]{:S(2)}) async-start(), calls=%async_computation.5 | async-start | bytes 5242880 | tf_op jit(solution)/shard_map/all_gather | solution.py:63
Sparse Core Ops, SparseCore 0:
  114.1 65.2 reduce-scatter.1
  182.1 33.4 all-gather.1
where the time goes:
time: 228 us
  waiting for transfers between devices  106 us (46%)
  blocking collectives  74.8 us (33%)
  between operations  14.2 us (6%)
  matrix products  12.1 us (5%)
  local copies, waits for them, and re-layouts  8.48 us (4%)
  starting transfers between devices  7.28 us (3%)
  other arithmetic  4.87 us (2%)
    reduce_scatter x1, waiting for transfers between devices, on_device(): lax.psum_scatter(partial_count, 'snap', scatter_dimension=0, tiled=True)  68.1 us
    all_to_all x1, blocking collectives, on_device(): lax.all_to_all(shaped, 'snap', split_axis=2, concat_axis=3, tiled=True)  55.3 us
    all_gather x1, waiting for transfers between devices, on_device(): lax.all_gather(correl, 'ord', axis=0, tiled=True)  33.6 us
    unnamed x1, blocking collectives  19.4 us
    dot_general x1, matrix products, on_device(): jnp.einsum('ka,sqa->ksq', dft_table, images, preferred_element_type=jnp.f...  5.75 us
  transfers between devices with their start and end apart: 4, of which 3 were waited for; matrix products, arithmetic and copies ran while one was open for 1% of the time, Pallas kernels for 0%

commit v1 on v0

v1 whole, which is shorter than its diff:
```python
import math

import jax
import jax.numpy as jnp
import numpy as np
from jax import lax
from jax.sharding import Mesh, PartitionSpec as P

HALVES = 2
SNAP = ("high", "low")
ORD = ("x", "core")
GRAM_SCALE = 2.0**33
KAM_SCALE = 2.0**38


def make_table(orders, angles):
    order_index = np.arange(orders)[:, None]
    angle_index = np.arange(angles)[None, :]
    phase_index = (order_index * angle_index) % angles
    radians = phase_index.astype(np.float32) * np.float32(2.0 * math.pi / angles)
    norming = np.float32(math.sqrt(2.0 / angles))
    return np.stack([np.cos(radians) * norming, -np.sin(radians) * norming])


def encode(value, scale):
    scaled = value * scale
    return (scaled * jnp.abs(scaled)).astype(jnp.bfloat16)


def decode(code, scale):
    code = code.astype(jnp.float32)
    root = jnp.sqrt(jnp.abs(code)) * (1.0 / scale)
    return jnp.where(code < 0, -root, root)


def swap(value, axis, size, shift):
    return lax.ppermute(value, axis, [(at, (at + shift) % size) for at in range(size)])


def on_device(images, cycle_masks, weights, inversion):
    snap_dev, cycles, angles = images.shape
    orders = inversion.shape[0]
    low_size, x_size, core_size = (lax.axis_size(name) for name in ("low", "x", "core"))
    ord_size = x_size * core_size
    snap_size = HALVES * low_size
    x_index, core_index = lax.axis_index("x"), lax.axis_index("core")
    ord_index = x_index * core_size + core_index
    group = low_size * ord_size
    owned = orders // group
    rows = cycles // snap_size
    chip_orders = orders // x_size
    out_orders = orders // ord_size

    masks = cycle_masks.astype(jnp.float32)
    counts = jnp.einsum("sq,sp->qp", masks * weights[:, None], masks, precision=lax.Precision.HIGHEST)
    weight_row = jnp.zeros((1, cycles), jnp.float32).at[0, : weights.shape[0]].set(weights)
    early = jnp.concatenate(
        [
            counts.reshape(snap_size, rows, cycles),
            jnp.broadcast_to(weight_row[None], (snap_size, 1, cycles)),
        ],
        axis=1,
    )
    early = lax.all_to_all(early, SNAP, split_axis=0, concat_axis=0, tiled=True)
    pair_count = early[:, :rows].sum(0)
    half = early.reshape(HALVES, low_size, rows + 1, cycles)
    half = lax.dynamic_index_in_dim(half, lax.axis_index("high"), 0, keepdims=False)
    weight_half = half[:, rows, : weights.shape[0]].reshape(group, snap_dev)

    own_masks = lax.dynamic_slice_in_dim(masks, ord_index * snap_dev, snap_dev, 0)
    table = make_table(orders, angles).reshape(2, ord_size, low_size, owned, angles)
    table = table.transpose(2, 1, 0, 3, 4).reshape(2 * orders, angles)
    table = jnp.asarray(table).astype(jnp.bfloat16)
    coeffs = jnp.einsum("ka,sqa->ksq", table, images, preferred_element_type=jnp.float32)
    coeffs = (coeffs * own_masks[None]).astype(jnp.bfloat16)
    coeffs = coeffs.reshape(group, 2, owned, snap_dev, cycles)
    arrived = lax.all_to_all(coeffs, ("low", "x", "core"), split_axis=0, concat_axis=0, tiled=True)
    weighted = arrived.astype(jnp.float32) * weight_half[:, None, None, :, None]
    gram = jnp.einsum(
        "drnsq,drnsp->nqp", weighted.astype(jnp.bfloat16), arrived, preferred_element_type=jnp.float32
    )
    gram = encode(gram, GRAM_SCALE).reshape(owned, snap_size, rows, cycles).transpose(1, 0, 2, 3)
    gram = lax.all_to_all(gram, SNAP, split_axis=0, concat_axis=0, tiled=True)
    gram = decode(gram, GRAM_SCALE).reshape(HALVES, low_size * owned, rows, cycles).sum(0)
    other = swap(encode(gram, GRAM_SCALE), "core", core_size, 1)
    other = decode(other, GRAM_SCALE)
    own_part = lax.dynamic_slice_in_dim(inversion, x_index * chip_orders, chip_orders, 1)
    own_part = own_part.reshape(orders, core_size, out_orders)
    mine = lax.dynamic_index_in_dim(own_part, core_index, 1, keepdims=False)
    theirs = lax.dynamic_index_in_dim(own_part, 1 - core_index, 1, keepdims=False)
    norm = 1.0 / jnp.maximum(pair_count, 1.0)
    total = 0.0
    for shift in reversed(range(x_size)):
        target = ((x_index + shift) % x_size * core_size + core_index) * out_orders
        kam = sum(
            jnp.einsum(
                "ln,nqp->lqp",
                lax.dynamic_slice_in_dim(part, target, out_orders, 0),
                value,
                precision=lax.Precision.HIGHEST,
            )
            for part, value in ((mine, gram), (theirs, other))
        )
        kam = kam * norm[None]
        if shift:
            kam = decode(swap(encode(kam, KAM_SCALE), "x", x_size, shift), KAM_SCALE)
        total = total + kam
    return total


def solution(mesh):
    snap_size, ord_size = mesh.shape["snap"], mesh.shape["ord"]
    fine = Mesh(
        mesh.devices.reshape(HALVES, snap_size // HALVES, ord_size // 2, 2), SNAP + ORD
    )
    placed = (P(SNAP + ORD, None, None), P(SNAP, None), P(SNAP), P())
    return jax.shard_map(
        on_device, mesh=fine, in_specs=placed, out_specs=P(ORD, SNAP, None), check_vma=False
    )
```

time: 228 us -> 112 us (0.49)
  blocking collectives: 74.8 us -> 0 us
  waiting for transfers between devices: 106 us -> 66.8 us
  between operations: 14.2 us -> 0.16 us
  starting transfers between devices: 7.28 us -> 18.9 us
  matrix products: 12.1 us -> 15.2 us
  local copies, waits for them, and re-layouts: 8.48 us -> 5.49 us
    reduce_scatter x1 -> x0, waiting for transfers between devices: 68.1 us -> none  [on_device(): lax.psum_scatter(partial_count, 'snap', scatter_dimension=0, tiled=True)]
    all_to_all x1 -> x0, blocking collectives: 55.3 us -> none  [on_device(): lax.all_to_all(shaped, 'snap', split_axis=2, concat_axis=3, tiled=True)]
    all_to_all x2 -> x3, waiting for transfers between devices: 4.52 us -> 55.6 us  [the longest x1 28.9 us: on_device(): lax.all_to_all(coeffs, ('low', 'x', 'core'), split_axis=0, concat_axis=0,...]
    all_gather x1 -> x0, waiting for transfers between devices: 33.6 us -> none  [on_device(): lax.all_gather(correl, 'ord', axis=0, tiled=True)]
    unnamed x1 -> x0, blocking collectives: 19.4 us -> none
    ppermute x0 -> x2, waiting for transfers between devices: none -> 11.2 us  [swap(): lax.ppermute(value, axis, [(at, (at + shift) % size) for at in range(size)])]
    all_to_all x2 -> x3, starting transfers between devices: 7.2 us -> 17.3 us  [the longest x1 7.31 us: on_device(): early = lax.all_to_all(early, SNAP, split_axis=0, concat_axis=0, tiled=True)]
    reshape x1 -> x2, local copies, waits for them, and re-layouts: 0.09 us -> 3.6 us  [the longest x1 2.54 us: on_device(): coeffs = coeffs.reshape(group, 2, owned, snap_dev, cycles)]
  transfers between devices with their start and end apart: 4 -> 5, of which waited for: 3 -> 5; matrix products, arithmetic and copies ran while one was open for 1% -> 12% of each run, Pallas kernels for 0% -> 0%
where the time goes in v1:
time: 112 us
  waiting for transfers between devices  66.8 us (60%)
  starting transfers between devices  18.9 us (17%)
  matrix products  15.2 us (14%)
  local copies, waits for them, and re-layouts  5.49 us (5%)
  other arithmetic  5.27 us (5%)
    all_to_all x1, waiting for transfers between devices, on_device(): lax.all_to_all(coeffs, ('low', 'x', 'core'), split_axis=0, concat_axis=0,...  28.9 us
    all_to_all x1, waiting for transfers between devices, on_device(): gram = lax.all_to_all(gram, SNAP, split_axis=0, concat_axis=0, tiled=True)  25.8 us
    ppermute x2, waiting for transfers between devices, swap(): lax.ppermute(value, axis, [(at, (at + shift) % size) for at in range(size)])  11.2 us
    all_to_all x1, starting transfers between devices, on_device(): early = lax.all_to_all(early, SNAP, split_axis=0, concat_axis=0, tiled=True)  7.31 us
    dot_general x4, matrix products, on_device(): jnp.einsum('ln,nqp->lqp', lax.dynamic_slice_in_dim(part, target, out_orde...  6.8 us
    dot_general x1, matrix products, on_device(): jnp.einsum('ka,sqa->ksq', table, images, preferred_element_type=jnp.float32)  5.93 us
    all_to_all x1, starting transfers between devices, on_device(): gram = lax.all_to_all(gram, SNAP, split_axis=0, concat_axis=0, tiled=True)  5.69 us
    all_to_all x1, starting transfers between devices, on_device(): lax.all_to_all(coeffs, ('low', 'x', 'core'), split_axis=0, concat_axis=0,...  4.27 us
  transfers between devices with their start and end apart: 5, of which 5 were waited for; matrix products, arithmetic and copies ran while one was open for 12% of the time, Pallas kernels for 0%

profile of v1, /device:TPU:0, one launch (start us, length us, event | category | flops | bytes accessed | tf_op | source)
XLA Modules:
  0.0 111.8 jit_solution(732928158531198159)
XLA Ops:
  0.0 0.0 copy-start
  0.0 0.6 compare_reduce_fusion
  0.6 1.3 %broadcast_select_fusion = f32[64]{0:T(128)S(1)} fusion(f32[64]{0:T(128)} %param.9, pred[]{:T(512)} %compare_reduce_fusion), kind=kLoop, calls=%fused_computation.65 | loop fusion | flops 64 | bytes 513 | tf_op jit(solution)/shard_map/broadcast_in_dim | solution.py:60
  1.9 1.4 %fusion.23 = f32[256,256]{1,0:T(8,128)S(1)} fusion(f32[64]{0:T(128)} %param.9, s32[64,256]{1,0:T(8,128)} %param.8), kind=kOutput, calls=%fused_computation.45 | convolution fusion | flops 50380800 | bytes 327936 | tf_op jit(solution)/shard_map/sq,sp->qp/dot_general | solution.py:55
  3.4 0.8 pad_maximum_fusion
  4.1 7.3 %all-to-all-start.1 = ((f32[8,33,256]{2,1,0:T(8,128)}), f32[8,33,256]{2,1,0:T(8,128)S(1)}, u32[]{:S(2)}, u32[]{:S(2)}) async-start(f32[8,33,256]{2,1,0:T(8,128)} %pad_maximum_fusion), calls=%async_computation.1 | async-start | bytes 655360 | tf_op jit(solution)/shard_map/all_to_all | solution.py:64
  11.4 0.8 convert_element_type.34
  12.3 5.9 %multiply_convert_fusion.1 = bf16[256,16,256]{2,0,1:T(8,128)(2,1)S(1)} fusion(bf16[256,1024,1]{1,0,2:T(8,128)(2,1)} %constant.169, bf16[16,256,1024]{2,1,0:T(8,128)(2,1)} %param.7, f32[16,256]{1,0:T(8,128)S(1)} %constant_dynamic-slice_fusion.1), kind=kOutput, calls=%fused_computation.1 | convolution fusion | flops 2149580800 | bytes 11026432 | tf_op jit(solution)/shard_map/ka,sqa->ksq/dot_general | solution.py:74
  18.2 2.5 %copy.27 = bf16[16,2,8,16,256]{4,3,1,2,0:T(8,128)(2,1)} copy(bf16[16,2,8,16,256]{4,2,1,0,3:T(8,128)(2,1)S(1)} %bitcast.47) | data formatting | bytes 4194304 | tf_op jit(solution)/shard_map/reshape | solution.py:76
  20.8 1.0 all-to-all-done.1
  21.7 4.3 %all-to-all-start = ((bf16[16,2,8,16,256]{4,3,1,2,0:T(8,128)(2,1)}), bf16[16,2,8,16,256]{4,3,1,2,0:T(8,128)(2,1)S(1)}, u32[]{:S(2)}, u32[]{:S(2)}) async-start(bf16[16,2,8,16,256]{4,3,1,2,0:T(8,128)(2,1)} %copy.27), calls=%async_computation | async-start | bytes 4194304 | tf_op jit(solution)/shard_map/all_to_all | solution.py:77
  26.0 0.1 copy.49
  26.1 0.1 mul.115
  26.2 28.9 %all-to-all-done = bf16[16,2,8,16,256]{4,3,1,2,0:T(8,128)(2,1)S(1)} async-done(((bf16[16,2,8,16,256]{4,3,1,2,0:T(8,128)(2,1)}), bf16[16,2,8,16,256]{4,3,1,2,0:T(8,128)(2,1)S(1)}, u32[]{:S(2)}, u32[]{:S(2)}) %all-to-all-start) | async-done | bytes 2097184 | tf_op jit(solution)/shard_map/all_to_all | solution.py:77
  55.1 1.0 fusion.3
  56.1 1.1 copy.48
  57.2 5.7 %all-to-all-start.2 = ((bf16[8,8,32,256]{3,2,1,0:T(8,128)(2,1)}), bf16[8,8,32,256]{3,2,1,0:T(8,128)(2,1)S(1)}, u32[]{:S(2)}, u32[]{:S(2)}) async-start(bf16[8,8,32,256]{3,2,1,0:T(8,128)(2,1)} %bitcast.43), calls=%async_computation.2 | async-start | bytes 2097152 | tf_op jit(solution)/shard_map/all_to_all | solution.py:83
  62.9 0.0 copy-done
  62.9 0.1 constant_dynamic-slice_fusion.2
  63.0 0.1 copy.39
  63.0 25.8 %all-to-all-done.2 = bf16[8,8,32,256]{3,2,1,0:T(8,128)(2,1)S(1)} async-done(((bf16[8,8,32,256]{3,2,1,0:T(8,128)(2,1)}), bf16[8,8,32,256]{3,2,1,0:T(8,128)(2,1)S(1)}, u32[]{:S(2)}, u32[]{:S(2)}) %all-to-all-start.2) | async-done | bytes 1048608 | tf_op jit(solution)/shard_map/all_to_all | solution.py:83
  88.8 0.9 negate_select_fusion
  89.7 0.2 bitcast_reduce_fusion
  89.9 0.6 fusion.13
  90.5 0.1 collective-permute-start
  90.7 1.6 %fusion.17 = f32[32,32,256]{2,0,1:T(8,128)S(1)} fusion(f32[32,32,256]{2,1,0:T(8,128)S(1)} %bitcast_reduce_fusion, f32[128,2,32]{0,2,1:T(8,128)S(1)} %bitcast.52, s32[]{:T(128)S(6)} %select_n.58, s32[]{:T(128)S(6)} %select_n.60), kind=kOutput, calls=%fused_computation.36 | convolution fusion | flops 100663296 | bytes 2113544 | tf_op jit(solution)/shard_map/ln,nqp->lqp/dot_general | solution.py:96
  92.3 0.2 collective-permute-done
  92.5 1.6 %fusion.8 = bf16[32,32,256]{2,0,1:T(8,128)(2,1)S(1)} fusion(f32[32,32,256]{2,0,1:T(8,128)S(1)} %fusion.17, bf16[32,32,256]{2,0,1:T(8,128)(2,1)S(1)} %collective-permute-done, f32[32,256]{1,0:T(8,128)S(1)} %maximum_divide_fusion, f32[128,2,32]{0,2,1:T(8,128)S(1)} %bitcast.53, s32[]{:T(128)S(6)} %select_n.58, s32[]{:T(128)S(6)} %select_n.65), kind=kOutput, calls=%fused_computation.26 | convolution fusion | flops 103809024 | bytes 2146312 | tf_op jit(solution)/shard_map/ln,nqp->lqp/dot_general | solution.py:96
  94.1 1.6 %collective-permute-start.1 = (bf16[32,32,256]{2,0,1:T(8,128)(2,1)S(1)}, bf16[32,32,256]{2,0,1:T(8,128)(2,1)S(1)}, u32[]{:S(2)}, u32[]{:S(2)}) collective-permute-start(bf16[32,32,256]{2,0,1:T(8,128)(2,1)S(1)} %fusion.8), channel_id=1, source_target_pairs={{0,2},{2,0},{1,3},{3,1},{4,6},{6,4},{5,7},{7,5},{8,10},{10,8},{9,1... | collective-permute-start | bytes 1572872 | tf_op jit(solution)/shard_map/ppermute | solution.py:37
  95.7 1.6 %fusion.15 = f32[32,32,256]{2,0,1:T(8,128)S(1)} fusion(f32[32,32,256]{2,1,0:T(8,128)S(1)} %bitcast_reduce_fusion, f32[128,2,32]{0,2,1:T(8,128)S(1)} %bitcast.54, s32[]{:T(128)S(6)} %select_n.70, s32[]{:T(128)S(6)} %select_n.60), kind=kOutput, calls=%fused_computation.34 | convolution fusion | flops 100663296 | bytes 2113544 | tf_op jit(solution)/shard_map/ln,nqp->lqp/dot_general | solution.py:96
  97.3 11.0 %collective-permute-done.1 = bf16[32,32,256]{2,0,1:T(8,128)(2,1)S(1)} collective-permute-done((bf16[32,32,256]{2,0,1:T(8,128)(2,1)S(1)}, bf16[32,32,256]{2,0,1:T(8,128)(2,1)S(1)}, u32[]{:S(2)}, u32[]{:S(2)}) %collective-permute-start.1) | collective-permute-done | bytes 524320 | tf_op jit(solution)/shard_map/ppermute | solution.py:37
  108.3 1.9 %fusion.14 = f32[32,32,256]{2,0,1:T(8,128)S(1)} fusion(bf16[32,32,256]{2,0,1:T(8,128)(2,1)S(1)} %collective-permute-done.1, f32[32,32,256]{2,0,1:T(8,128)S(1)} %fusion.15, bf16[32,32,256]{2,0,1:T(8,128)(2,1)S(1)} %collective-permute-done, f32[32,256]{1,0:T(8,128)S(1)} %maximum_divide_fusion, f32[128,2,32]{0,2,1:T(8,128)S(1)} %bitcast.55, s32[]{:T(128)S(6)} %select_n.70, ...), kind=kOutput, calls=%fused_computation.32 | convolution fusion | flops 104595456 | bytes 3194888 | tf_op jit(solution)/shard_map/ln,nqp->lqp/dot_general | solution.py:96
  110.3 1.6 %copy.36 = f32[32,32,256]{2,1,0:T(8,128)} copy(f32[32,32,256]{2,0,1:T(8,128)S(1)} %fusion.14) | data formatting | bytes 2097152 | tf_op jit(solution)/shard_map/add | solution.py:107
  (7 shorter events, 0.1 us)
Async XLA Ops:
  0.0 62.9 %copy-start = (f32[128,128]{1,0:T(8,128)S(1)}, f32[128,128]{1,0:T(8,128)}, u32[]{:S(2)}) copy-start(f32[128,128]{1,0:T(8,128)} %param.10) | copy-start | bytes 196612
  4.1 17.6 %all-to-all-start.1 = ((f32[8,33,256]{2,1,0:T(8,128)}), f32[8,33,256]{2,1,0:T(8,128)S(1)}, u32[]{:S(2)}, u32[]{:S(2)}) async-start(f32[8,33,256]{2,1,0:T(8,128)} %pad_maximum_fusion), calls=%async_computation.1 | async-start | bytes 655360 | tf_op jit(solution)/shard_map/all_to_all | solution.py:64
  21.7 33.3 %all-to-all-start = ((bf16[16,2,8,16,256]{4,3,1,2,0:T(8,128)(2,1)}), bf16[16,2,8,16,256]{4,3,1,2,0:T(8,128)(2,1)S(1)}, u32[]{:S(2)}, u32[]{:S(2)}) async-start(bf16[16,2,8,16,256]{4,3,1,2,0:T(8,128)(2,1)} %copy.27), calls=%async_computation | async-start | bytes 4194304 | tf_op jit(solution)/shard_map/all_to_all | solution.py:77
  57.2 31.6 %all-to-all-start.2 = ((bf16[8,8,32,256]{3,2,1,0:T(8,128)(2,1)}), bf16[8,8,32,256]{3,2,1,0:T(8,128)(2,1)S(1)}, u32[]{:S(2)}, u32[]{:S(2)}) async-start(bf16[8,8,32,256]{3,2,1,0:T(8,128)(2,1)} %bitcast.43), calls=%async_computation.2 | async-start | bytes 2097152 | tf_op jit(solution)/shard_map/all_to_all | solution.py:83
  90.5 2.0 %collective-permute-start = (bf16[32,32,256]{2,0,1:T(8,128)(2,1)S(1)}, bf16[32,32,256]{2,0,1:T(8,128)(2,1)S(1)}, u32[]{:S(2)}, u32[]{:S(2)}) collective-permute-start(bf16[32,32,256]{2,0,1:T(8,128)(2,1)S(1)} %fusion.13), channel_id=1, source_target_pairs={{0,1},{1,0},{2,3},{3,2},{4,5},{5,4},{6,7},{7,6},{8,9},{9,8},{10,11... | collective-permute-start | bytes 1572872 | tf_op jit(solution)/shard_map/ppermute | solution.py:37
  94.1 14.2 %collective-permute-start.1 = (bf16[32,32,256]{2,0,1:T(8,128)(2,1)S(1)}, bf16[32,32,256]{2,0,1:T(8,128)(2,1)S(1)}, u32[]{:S(2)}, u32[]{:S(2)}) collective-permute-start(bf16[32,32,256]{2,0,1:T(8,128)(2,1)S(1)} %fusion.8), channel_id=1, source_target_pairs={{0,2},{2,0},{1,3},{3,1},{4,6},{6,4},{5,7},{7,5},{8,10},{10,8},{9,1... | collective-permute-start | bytes 1572872 | tf_op jit(solution)/shard_map/ppermute | solution.py:37
